TPU v7x, 256 devices: a whole 4x4x8 slice. The times are simulated.
256 devices in a mesh: band: 32 (over x_hi, z, core), var: 8 (over y, x_lo).
Axes of the slice: x: 4 (x_hi: 2, x_lo: 2; x = x_hi * 2 + x_lo), y: 4, z: 8, core: 2. Of those that a mesh axis runs over, the one named last changes fastest.
Arguments:
- patches: bfloat16 [16, 32, 256, 64], P('var', 'band'), may hold values from -6 to 6
- w_embed: bfloat16 [16, 64, 2048], P('var'), may hold values from -0.75 to 0.75
- var_bias: float32 [16, 2048], P('var'), may hold values from -3 to 3
- agg_gain: float32 [2048], replicated, may hold values from 0.1 to 1.9
- wq: bfloat16 [2048, 2048], P(None, 'var'), may hold values from -4 to 4
- wk: bfloat16 [2048, 2048], P(None, 'var'), may hold values from -4 to 4
- wv: bfloat16 [2048, 2048], P(None, 'var'), may hold values from -0.125 to 0.125
- wo: bfloat16 [2048, 2048], P('var'), may hold values from -0.125 to 0.125
- w_up: bfloat16 [2048, 1024], replicated, may hold values from -0.125 to 0.125
- conv1: bfloat16 [9, 64, 64], replicated, may hold values from -0.25 to 0.25
- bias1: float32 [64], replicated, may hold values from -3 to 3
- conv2: bfloat16 [9, 64, 64], replicated, may hold values from -0.25 to 0.25
- cotangent: bfloat16 [128, 64, 1024], P('band', None, 'var'), may hold values from -6 to 6
Outputs:
- field_out: bfloat16 [128, 64, 1024], P('band', None, 'var')
- grad_fine: bfloat16 [128, 64, 1024], P('band', None, 'var')
- grad_conv1: float32 [9, 64, 64], replicated
- grad_conv2: float32 [9, 64, 64], replicated
- grad_bias: float32 [64], replicated
All inputs are finite; a program needn't handle non-finite values.
Results may differ from a plain program's by a relative error of at most 0.03.
Values may be sent and summed in bfloat16 or wider, within the bound.
No kernel may reach another device: no remote copies, remote signals or barrier semaphores. Data moves between devices by JAX's collectives and lax.ppermute only.
A program may use at most 128 MiB of HBM per device.

v0:
```python
import math

import jax
import jax.numpy as jnp
import numpy as np
from jax import lax
from jax.experimental import pallas as pl
from jax.experimental.pallas import tpu as pltpu
from jax.sharding import Mesh, PartitionSpec as P


D = 2048
HD = 128
C = 64
BAND = ("xh", "z", "core")
VAR = ("y", "xl")
BOARD = ("core", "y", "xl")
BF = jnp.bfloat16
F32 = jnp.float32
VMEM_SPEC = pl.BlockSpec(memory_space=pltpu.VMEM)
SMEM_SPEC = pl.BlockSpec(memory_space=pltpu.SMEM)
SCORE_SCALE = math.log2(math.e) / math.sqrt(HD)


def dot_nn(a, b):
    return lax.dot_general(a, b, (((1,), (0,)), ((), ())), preferred_element_type=F32)


def dot_nt(a, b):
    return lax.dot_general(a, b, (((1,), (1,)), ((), ())), preferred_element_type=F32)


def dot_tn(a, b):
    return lax.dot_general(a, b, (((0,), (0,)), ((), ())), preferred_element_type=F32)


def near(x):
    return pltpu.with_memory_space_constraint(x, pltpu.VMEM)


def mix_body(patches, weights, offsets, out):
    offset = offsets[0:1, :] + offsets[1:2, :]
    out[...] = (dot_tn(patches[...], weights[...]) + offset).astype(BF)


def mix(patches, weights, offsets):
    args = [pltpu.with_memory_space_constraint(x, pltpu.HBM) for x in (patches, weights, offsets)]
    return pl.pallas_call(
        mix_body,
        grid=(2,),
        out_shape=jax.ShapeDtypeStruct((256, D), BF),
        in_specs=[
            pl.BlockSpec((128, 256), lambda k: (0, 0)),
            pl.BlockSpec((128, 1024), lambda k: (0, k)),
            pl.BlockSpec((2, 1024), lambda k: (0, k)),
        ],
        out_specs=pl.BlockSpec((256, 1024), lambda k: (0, k)),
        compiler_params=pltpu.CompilerParams(vmem_limit_bytes=12 * 2**20),
        name="mix_variables",
    )(*args)


def residual_body(slab, weights, out):
    out[...] = dot_nn(slab[...], weights[...])


def residual(slab, weights):
    return pl.pallas_call(
        residual_body,
        grid=(4,),
        out_shape=jax.ShapeDtypeStruct((32, 1024), F32),
        in_specs=[
            pl.BlockSpec((32, D), lambda k: (0, 0)),
            pl.BlockSpec((D, 256), lambda k: (0, k)),
        ],
        out_specs=pl.BlockSpec((32, 256), lambda k: (0, k)),
        compiler_params=pltpu.CompilerParams(vmem_limit_bytes=12 * 2**20),
        name="residual_up",
    )(slab, pltpu.with_memory_space_constraint(weights, pltpu.HBM))


def norm_body(pieces, gain, out, slab):
    total = pieces[0].astype(F32)
    for k in range(1, 8):
        total = total + pieces[k].astype(F32)
    scale = lax.rsqrt(jnp.mean(total * total, axis=1, keepdims=True) + 1e-05)
    normed = (total * scale * gain[...]).astype(BF)
    slab[...] = normed
    for k in range(8):
        out[k] = normed


def norm_copies(pieces, gain):
    return pl.pallas_call(
        norm_body,
        out_shape=[pltpu.VMEM((8, 32, D), BF), pltpu.VMEM((32, D), BF)],
        in_specs=[VMEM_SPEC] * 2,
        out_specs=[VMEM_SPEC] * 2,
        compiler_params=pltpu.CompilerParams(vmem_limit_bytes=12 * 2**20),
        name="norm_slab",
    )(near(pieces), near(gain))


def flash_kernel(blocks, chunks, first, last):
    def body(*refs):
        q_refs = refs[:blocks]
        kv_refs = refs[blocks : blocks + chunks]
        rest = refs[blocks + chunks :]
        if not first:
            stat_in, acc_in = rest[0], rest[1]
            rest = rest[2:]
        if last:
            stat_scr, acc_scr, whole = rest[blocks], rest[blocks + 1], rest[blocks + 2]
            for k in range(chunks):
                whole[k * 128 : (k + 1) * 128, :] = kv_refs[k][...]
            kv_refs = [whole]
        for block in range(blocks):
            for part in range(2):
                inner = slice(part * 128, (part + 1) * 128)
                cols = slice(block * 256 + part * 128, block * 256 + (part + 1) * 128)
                for h in range(2):
                    head = slice(h * HD, (h + 1) * HD)
                    vals = slice(256 + h * HD, 256 + (h + 1) * HD)
                    q = q_refs[block][inner, head]
                    state = None
                    if not first:
                        state = (
                            stat_in[h : h + 1, cols],
                            stat_in[2 + h : 3 + h, cols],
                            acc_in[head, cols],
                        )
                    for kv in kv_refs:
                        s = dot_nt(kv[:, head], q) * SCORE_SCALE
                        top = jnp.max(s, axis=0, keepdims=True)
                        if state is not None:
                            top = jnp.maximum(top, state[0])
                        w = jnp.exp2(s - top)
                        total = jnp.sum(w, axis=0, keepdims=True)
                        update = dot_tn(kv[:, vals], w.astype(BF))
                        if state is not None:
                            shrink = jnp.exp2(state[0] - top)
                            total = total + state[1] * shrink
                            update = update + state[2] * shrink
                        state = (top, total, update)
                    top, total, update = state
                    if last:
                        acc_scr[head, cols] = update
                        stat_scr[h : h + 1, cols] = top
                        stat_scr[2 + h : 3 + h, cols] = total
                    else:
                        rest[1][head, cols] = update
                        rest[0][h : h + 1, cols] = top
                        rest[0][2 + h : 3 + h, cols] = total
        if last:
            rows = []
            for r in (0, 2, 1, 3):
                value = stat_scr[r : r + 1, :]
                high = value.astype(BF).astype(F32)
                mid = (value - high).astype(BF).astype(F32)
                rows += [high, mid, value - high - mid]
            rows.append(jnp.zeros((4, 256 * blocks), F32))
            tail = jnp.concatenate(rows, axis=0).astype(BF)
            for block in range(blocks):
                cols = slice(block * 256, (block + 1) * 256)
                rest[block][0:256, :] = acc_scr[:, cols].astype(BF)
                rest[block][256:272, :] = tail[:, cols]

    return body


def flash_step(queries, chunks, carry, last):
    blocks = len(queries)
    first = carry is None
    ins = list(queries) + list(chunks) + ([] if first else list(carry))
    if last:
        outs = [pltpu.VMEM((272, 256), BF)] * blocks
    else:
        outs = [
            pltpu.VMEM((8, 256 * blocks), F32),
            pltpu.VMEM((256, 256 * blocks), F32),
        ]
    return pl.pallas_call(
        flash_kernel(blocks, len(chunks), first, last),
        out_shape=outs,
        in_specs=[VMEM_SPEC] * len(ins),
        out_specs=[VMEM_SPEC] * len(outs),
        scratch_shapes=[
            pltpu.VMEM((8, 256 * blocks), F32),
            pltpu.VMEM((256, 256 * blocks), F32),
            pltpu.VMEM((256, 512), BF),
        ]
        if last
        else [],
        compiler_params=pltpu.CompilerParams(vmem_limit_bytes=12 * 2**20),
        name="flash_last" if last else "flash_step",
    )(*[near(x) for x in ins])


def merge_body(place, base, edges, b0, b1, b2, b3, mat, out):
    parts = (b0, b1, b2, b3)
    tails = [b[256:272, :].astype(F32) for b in parts]
    context = []
    for h in range(2):
        head = slice(h * HD, (h + 1) * HD)

        def whole(tail, row):
            return tail[row : row + 1] + tail[row + 1 : row + 2] + tail[row + 2 : row + 3]

        tops = [whole(tail, 6 * h) for tail in tails]
        top = jnp.maximum(jnp.maximum(tops[0], tops[1]), jnp.maximum(tops[2], tops[3]))
        ws = [jnp.exp2(v - top) for v in tops]
        total = sum(whole(tail, 6 * h + 3) * w for tail, w in zip(tails, ws))
        share = 1.0 / total
        mixed = sum(b[head, :].astype(F32) * (w * share) for b, w in zip(parts, ws))
        context.append(mixed.astype(BF))
    up = dot_tn(jnp.concatenate(context, axis=0), mat[...])
    own = place[0]
    sides = edges[...].astype(F32)
    for j in range(8):
        lower = jnp.where(own == j - 1, base[31:32, :], 0.0)
        upper = jnp.where(own == j + 1, base[0:1, :], 0.0)
        for half in range(2):
            rows = []
            for k in range(4):
                lanes = slice((half * 4 + k) * 128, (half * 4 + k + 1) * 128)
                out[j, half, k * 32 : (k + 1) * 32, :] = up[32 * j : 32 * j + 32, lanes].astype(BF)
                token = 32 * j + 32 if k % 2 == 0 else 32 * j - 1
                edge = upper if k % 2 == 0 else lower
                if 0 <= token < 256:
                    rows.append(up[token : token + 1, lanes] + edge[:, lanes])
                else:
                    rows.append(jnp.zeros((1, 128), F32))
            source = j - 1 if half == 0 else j + 1
            rows.append(jnp.where(own == source, sides[4 * half : 4 * half + 4], 0.0))
            rows.append(jnp.zeros((8, 128), F32))
            out[j, half, 128:144, :] = jnp.concatenate(rows, axis=0).astype(BF)


def merge(place, base, edges, parts, mat):
    return pl.pallas_call(
        merge_body,
        out_shape=pltpu.VMEM((8, 2, 144, 128), BF),
        in_specs=[SMEM_SPEC] + [VMEM_SPEC] * 7,
        out_specs=VMEM_SPEC,
        compiler_params=pltpu.CompilerParams(vmem_limit_bytes=12 * 2**20),
        name="merge_heads",
    )(place, near(base), near(edges), *[near(x) for x in parts], near(mat))


def collect_body(flags, pieces, base, grad, own, near_out, far_out):
    for half in range(2):
        total = pieces[0, half].astype(F32)
        for k in range(1, 8):
            total = total + pieces[k, half].astype(F32)
        own[half, 0:128, :] = (total[0:128] + base[half]).astype(BF)
        own[half, 128:144, :] = total[128:144].astype(BF)
    core = flags[4]
    for side, out in ((1 - core, near_out), (core, far_out)):
        out[0:144, :] = own[side]
        out[144:160, :] = own[1 - side, 128:144, :]
        for k in range(2):
            out[160 + 64 * k : 224 + 64 * k, :] = grad[2 * side + k]


def collect(flags, pieces, base, grad):
    return pl.pallas_call(
        collect_body,
        out_shape=[
            pltpu.VMEM((2, 144, 128), BF),
            pltpu.VMEM((288, 128), BF),
            pltpu.VMEM((288, 128), BF),
        ],
        in_specs=[SMEM_SPEC] + [VMEM_SPEC] * 3,
        out_specs=[VMEM_SPEC] * 3,
        compiler_params=pltpu.CompilerParams(vmem_limit_bytes=12 * 2**20),
        name="collect_slab",
    )(flags, near(pieces), near(base), near(grad))


def spread_matrix():
    spread = np.zeros((144, 2, 2, 256), np.float32)
    for a in range(2):
        for bh in range(2):
            k = 2 * a + bh
            for bl in range(2):
                for token in range(32):
                    spread[k * 32 + token, a, bl, 4 * token + 2 * bh + bl] = 1
                spread[128 + k, a, bl, (128 + bl) if bh == 0 else (254 + bl)] = 1
    return spread.reshape(144, 1024)


def edge_matrix():
    edges = np.zeros((2, 16, 2, 4, 128), np.float32)
    for q in range(2):
        for r in range(4):
            k, m = divmod(4 * q + r, 2)
            edges[0, 4 + k, m, r, 126 + q] = 1
            edges[1, 4 + k, m, r, q] = 1
    return edges.reshape(32, 1024)


def gelu_pair(x):
    root = math.sqrt(2.0 / math.pi)
    t = jnp.tanh(root * (x + 0.044715 * (x * x * x)))
    half = 0.5 * (1.0 + t)
    slope = half + 0.5 * x * (1.0 - t * t) * (root * (1.0 + 3 * 0.044715 * (x * x)))
    return x * half, slope


def shifted(row):
    return jnp.concatenate(
        [pltpu.roll(row, 1, 1), row, pltpu.roll(row, row.shape[1] - 1, 1)], axis=0
    )


def fine_body(factor):
    def body(flags, own, near_up, far_up, spread, edges, grad, mats, bias, field, grad_fine, terms):
        spread_all = spread[...]
        ups = []
        second_core = flags[4] > 0
        close, distant = near_up[...].astype(F32), far_up[...].astype(F32)
        prev = jnp.where(second_core, close, distant).astype(BF)
        nxt = jnp.where(second_core, distant, close).astype(BF)
        for block in (prev[0:144], own[0], own[1], nxt[0:144]):
            wide = dot_tn(block, spread_all)
            for a in range(2):
                ups.append(
                    wide[0:64, 512 * a : 512 * a + 256] + wide[64:128, 512 * a + 256 : 512 * a + 512]
                )
        edge_all = edges[...]
        rows_of = [
            [prev[160:224], prev[224:288]],
            [grad[r] for r in range(4)],
            [nxt[160:224], nxt[224:288]],
        ]
        lefts = [prev[144:160], own[0, 128:144, :], nxt[128:144]]
        rights = [prev[128:144], own[1, 128:144, :], nxt[144:160]]
        grads = []
        for k in range(3):
            wide = dot_tn(jnp.concatenate([lefts[k], rights[k]], axis=0), edge_all)
            for r, row in enumerate(rows_of[k]):
                at = (r + 2 if k == 0 else r) * 128
                rim = wide[0:64, at : at + 128] + wide[64:128, 512 + at : 640 + at]
                grads.append(jnp.concatenate([row.astype(F32), rim], axis=1))
        up_taps = [shifted(u).astype(BF) for u in ups]
        grad_taps = [shifted(g).astype(BF) for g in grads]
        pre_all = dot_nn(mats[0], jnp.concatenate(up_taps, axis=1))
        act_all = dot_nn(mats[1], jnp.concatenate(grad_taps, axis=1))

        def gather(products, i, width):
            return (
                products[0:64, i * width : (i + 1) * width]
                + products[64:128, (i + 1) * width : (i + 2) * width]
                + products[128:192, (i + 2) * width : (i + 3) * width]
            )

        lane = lax.broadcasted_iota(jnp.int32, (64, 256), 1)
        cols_ok = (lane < 128) | ((lane == 128) & (flags[3] > 0)) | ((lane == 255) & (flags[2] > 0))
        offset = bias[...]
        act_taps = []
        pre_taps = []
        d_rows = []
        for i in range(6):
            pre = gather(pre_all, i, 256) + offset
            value, slope = gelu_pair(pre)
            ok = cols_ok
            if i == 0:
                ok = ok & (flags[0] > 0)
            if i == 5:
                ok = ok & (flags[1] > 0)
            value = jnp.where(ok, value, 0.0)
            d_pre = jnp.where(ok, gather(act_all, i, 256) * slope, 0.0)
            act_taps.append(shifted(value)[:, 0:128].astype(BF))
            pre_taps.append(shifted(d_pre)[:, 0:128].astype(BF))
            if 1 <= i <= 4:
                d_rows.append(d_pre[:, 0:128].astype(BF))
        act_wide = jnp.concatenate(act_taps, axis=1)
        out_all = dot_nn(mats[2], act_wide)
        fine_all = dot_nn(mats[3], jnp.concatenate(pre_taps, axis=1))
        for j in range(4):
            field[j] = (
                gather(out_all, j, 128) + ups[j + 2][:, 0:128]
            ).astype(BF)
            grad_fine[j] = (gather(fine_all, j, 128) + grads[j + 2][:, 0:128]).astype(BF)
        d_own = jnp.concatenate(d_rows, axis=1)
        g_own = jnp.concatenate([grad[r] for r in range(4)], axis=1)
        for p in range(3):
            up_cut = jnp.concatenate([up_taps[r][:, 0:128] for r in range(p + 1, p + 5)], axis=1)
            first = dot_nt(up_cut, d_own)
            second = dot_nt(act_wide[:, p * 128 : p * 128 + 512], g_own)
            terms[p * 192 : (p + 1) * 192, :] = (
                jnp.concatenate([first, second], axis=1) * factor
            ).astype(BF)
        ones = jnp.ones((16, 512), BF)
        third = dot_nt(ones, d_own) * factor
        terms[576:592, :] = jnp.concatenate([third, jnp.zeros((16, 64), F32)], axis=1).astype(BF)
        terms[592:768, :] = jnp.zeros((176, 128), BF)

    return body


def fine_stage(flags, own, near_up, far_up, spread, edges, grad, mats, bias, factor):
    return pl.pallas_call(
        fine_body(factor),
        out_shape=[
            jax.ShapeDtypeStruct((4, 64, 128), BF),
            jax.ShapeDtypeStruct((4, 64, 128), BF),
            pltpu.VMEM((768, 128), BF),
        ],
        in_specs=[SMEM_SPEC] + [VMEM_SPEC] * 8,
        out_specs=[VMEM_SPEC] * 3,
        compiler_params=pltpu.CompilerParams(vmem_limit_bytes=20 * 2**20),
        name="fine_stage",
    )(flags, *[near(x) for x in (own, near_up, far_up, spread, edges, grad, mats, bias)])


def finish_body(totals, first, second, third):
    first[...] = totals[0:576, 0:64].astype(F32)
    second[...] = totals[0:576, 64:128].astype(F32)
    third[...] = totals[576:592, 0:64].astype(F32)[0:1]


def finish(totals):
    return pl.pallas_call(
        finish_body,
        out_shape=[
            jax.ShapeDtypeStruct((576, 64), F32),
            jax.ShapeDtypeStruct((576, 64), F32),
            jax.ShapeDtypeStruct((1, 64), F32),
        ],
        in_specs=[VMEM_SPEC],
        out_specs=[VMEM_SPEC] * 3,
        compiler_params=pltpu.CompilerParams(vmem_limit_bytes=12 * 2**20),
        name="finish_grads",
    )(near(totals))


def copies(piece, axis, count):
    return lax.all_to_all(jnp.broadcast_to(piece[None], (count,) + piece.shape), axis, 0, 0)


def flip(count, bit):
    return [(i, i ^ bit) for i in range(count)]


def turn(count, step):
    return [(i, (i + step) % count) for i in range(count)]


def tap_matrix(weight):
    return jnp.transpose(weight.reshape(3, 3, C, C), (0, 3, 1, 2)).reshape(3 * C, 3 * C)


def flipped(weight):
    return jnp.transpose(weight[::-1], (0, 2, 1))


def device_step(
    patches, w_embed, var_bias, agg_gain, wq, wk, wv, wo, w_up, conv1, bias1, conv2, cotangent
):
    var_at = lax.axis_index(VAR)
    band_at = lax.axis_index(BAND)
    group = ("xh", "core")

    core_at = lax.axis_index("core")
    turned = jnp.transpose(patches, (0, 1, 3, 2)).reshape(128, 256)
    partial_mix = mix(turned, w_embed.reshape(128, D), var_bias).reshape(8, 32, D)
    partial_mix, wo, cells = lax.optimization_barrier((partial_mix, wo, cotangent))
    pieces = lax.all_to_all(partial_mix, VAR, 0, 0)
    up_mat = jnp.dot(wo, w_up, preferred_element_type=F32).astype(BF)
    edges = jnp.concatenate(
        [
            jnp.transpose(cells[:, :, at : at + 2], (2, 0, 1)).reshape(4, 128) for at in (126, 0)
        ],
        axis=0,
    )
    pieces, up_mat, edges = lax.optimization_barrier((pieces, up_mat, edges))
    spread_out, slab = norm_copies(pieces, agg_gain.reshape(1, D))
    normed = lax.all_to_all(spread_out, VAR, 0, 0).reshape(256, D)

    keyvals = jnp.concatenate(
        [jnp.dot(normed, w, preferred_element_type=F32).astype(BF) for w in (wk, wv)], axis=1
    )
    ahead = lax.ppermute(keyvals, "z", turn(8, 1))
    behind = lax.ppermute(keyvals, "z", turn(8, -1))
    queries = jnp.dot(normed, wq, preferred_element_type=F32).astype(BF)
    all_queries = [queries] + [lax.ppermute(queries, group, flip(4, k)) for k in (2, 3, 1)]
    fresh = [keyvals, ahead, behind]
    ahead = lax.ppermute(ahead, "z", turn(8, 1))
    behind = lax.ppermute(behind, "z", turn(8, -1))
    carry = flash_step(all_queries, fresh, None, False)
    ahead, behind, carry = lax.optimization_barrier((ahead, behind, carry))
    for step in (2, 3):
        fresh = [ahead, behind]
        if step == 3:
            ahead, behind = ahead[:128], behind[128:]
        ahead = lax.ppermute(ahead, "z", turn(8, 1))
        behind = lax.ppermute(behind, "z", turn(8, -1))
        carry = flash_step(all_queries, fresh, carry, False)
        ahead, behind, carry = lax.optimization_barrier((ahead, behind, carry))
    fresh = [ahead, behind]

    blocks = list(flash_step(all_queries, fresh, carry, True))
    blocks[0], slab, bias1 = lax.optimization_barrier((blocks[0], slab, bias1))
    base = residual(slab, w_up)
    bias = bias1.reshape(C, 1)
    flags = jnp.stack(
        [band_at > 0, band_at < 31, var_at > 0, var_at < 7, core_at > 0]
    ).astype(jnp.int32)
    parts = [blocks[0]] + [lax.ppermute(b, group, flip(4, k)) for b, k in zip(blocks[1:], (2, 3, 1))]
    place = var_at.reshape(1).astype(jnp.int32)
    merged = merge(place, base, edges, parts, up_mat)
    merged, conv1, conv2 = lax.optimization_barrier((merged, conv1, conv2))
    pieces = lax.all_to_all(merged, VAR, 0, 0)
    mats = jnp.stack(
        [tap_matrix(conv1), tap_matrix(flipped(conv2)), tap_matrix(conv2), tap_matrix(flipped(conv1))]
    )
    pieces, mats = lax.optimization_barrier((pieces, mats))
    base_main = jnp.transpose(base.reshape(32, 2, 4, 128), (1, 2, 0, 3)).reshape(2, 128, 128)
    up, near_rows, far_rows = collect(flags, pieces, base_main, cells)
    near_up = lax.ppermute(near_rows, "core", flip(2, 1))
    pairs = [(i, i + 1) for i in range(1, 31, 2)] + [(i + 1, i) for i in range(1, 31, 2)]
    far_up = lax.ppermute(far_rows, BAND, pairs)
    factor = 1.0 / math.sqrt(128 * 1024)
    spread = jnp.asarray(spread_matrix(), BF)
    field_out, grad_fine, terms = fine_stage(
        flags, up, near_up, far_up, spread, jnp.asarray(edge_matrix(), BF), cells, mats, bias, factor
    )
    shares = lax.all_to_all(terms.reshape(16, 48, 128), BOARD, 0, 0)
    share = jnp.sum(shares.astype(F32), axis=0).astype(BF)
    other = lax.ppermute(share, "xh", flip(2, 1))
    share = (share.astype(F32) + other.astype(F32)).astype(BF)
    share = jnp.sum(copies(share, "z", 8).astype(F32), axis=0).astype(BF)
    totals = copies(share, BOARD, 16).reshape(768, 128)
    first, second, third = finish(totals)
    return (field_out, grad_fine, first.reshape(9, C, C), second.reshape(9, C, C), third.reshape(C))


def solution(mesh):
    fine_mesh = Mesh(mesh.devices.reshape(2, 8, 2, 4, 2), BAND + VAR)
    in_specs = (
        P(VAR, BAND, None, None),
        P(VAR, None, None),
        P(VAR, None),
        P(),
        P(None, VAR),
        P(None, VAR),
        P(None, VAR),
        P(VAR, None),
        P(),
        P(),
        P(),
        P(),
        P(BAND, None, VAR),
    )
    out_specs = (P(BAND, None, VAR), P(BAND, None, VAR), P(), P(), P())
    return jax.shard_map(
        device_step, mesh=fine_mesh, in_specs=in_specs, out_specs=out_specs, check_vma=False
    )
```

profile of v0, /device:TPU:1, one launch (start us, length us, event | category | flops | bytes accessed | tf_op | source)
XLA Modules:
  0.0 167.8 jit_solution(2591279911679677505)
XLA Ops:
  0.6 2.6 %mix_variables.1 = bf16[256,2048]{1,0:T(8,128)(2,1)} custom-call(bf16[128,256]{1,0:T(8,128)(2,1)} %bitcast.66, bf16[128,2048]{1,0:T(8,128)(2,1)} %bitcast.65, f32[2,2048]{1,0:T(2,128)} %offsets.1), custom_call_target="tpu_custom_call" | custom-call | tf_op jit(solution)/shard_map/mix_variables/pallas_call | solution.py:48
  3.3 5.9 %all-to-all-start = ((bf16[8,32,2048]{2,1,0:T(8,128)(2,1)}), bf16[8,32,2048]{2,1,0:T(8,128)(2,1)S(1)}, u32[]{:S(2)}, u32[]{:S(2)}) async-start(bf16[8,32,2048]{2,1,0:T(8,128)(2,1)} %bitcast.9), calls=%async_computation | async-start | bytes 2097152 | tf_op jit(solution)/shard_map/all_to_all | solution.py:469
  10.6 3.4 %convolution_convert_fusion.mat = bf16[256,1024]{1,0:T(8,128)(2,1)S(1)} fusion(bf16[256,2048]{1,0:T(8,128)(2,1)S(1)} %copy-done, bf16[2048,1024]{1,0:T(8,128)(2,1)} %weights.1), kind=kOutput, calls=%fused_computation | convolution fusion | flops 1074003968 | bytes 5767168 | tf_op jit(solution)/shard_map/dot_general | solution.py:470
  14.1 9.7 %all-to-all-done.pieces = bf16[8,32,2048]{2,1,0:T(8,128)(2,1)S(1)} async-done(((bf16[8,32,2048]{2,1,0:T(8,128)(2,1)}), bf16[8,32,2048]{2,1,0:T(8,128)(2,1)S(1)}, u32[]{:S(2)}, u32[]{:S(2)}) %all-to-all-start) | async-done | bytes 1048608 | tf_op jit(solution)/shard_map/all_to_all | solution.py:469
  24.0 18.9 %all_to_all.30 = bf16[8,32,2048]{2,1,0:T(8,128)(2,1)S(1)} all-to-all(bf16[8,32,2048]{2,1,0:T(8,128)(2,1)S(1)} %get-tuple-element.56), channel_id=1, replica_groups=mesh['xh'=2,'z'=8,'core'=2,'y'=4,'xl'=2] {'y','xl'}, dimensions={0} | all-to-all | bytes 2097152 | tf_op jit(solution)/shard_map/all_to_all | solution.py:479
  45.0 1.7 %collective-permute-start.3 = (bf16[256,512]{1,0:T(8,128)(2,1)S(1)}, bf16[256,512]{1,0:T(8,128)(2,1)S(1)}, u32[]{:S(2)}, u32[]{:S(2)}) collective-permute-start(bf16[256,512]{1,0:T(8,128)(2,1)S(1)} %pad_maximum_fusion.1.refs_4_), channel_id=1, source_target_pairs={{0,16},{16,32},{32,48},{48,64},{64,80},{80,96},{96,112},{112,0},{1... | collective-permute-start | bytes 786440 | tf_op jit(solution)/shard_map/ppermute | solution.py:484
  46.7 4.0 %collective-permute-start.5 = (bf16[256,512]{1,0:T(8,128)(2,1)S(1)}, bf16[256,512]{1,0:T(8,128)(2,1)S(1)}, u32[]{:S(2)}, u32[]{:S(2)}) collective-permute-start(bf16[256,512]{1,0:T(8,128)(2,1)S(1)} %pad_maximum_fusion.1.refs_4_), channel_id=1, source_target_pairs={{0,112},{16,0},{32,16},{48,32},{64,48},{80,64},{96,80},{112,96},{1... | collective-permute-start | bytes 786440 | tf_op jit(solution)/shard_map/ppermute | solution.py:485
  50.8 4.7 %collective-permute-done.3.refs_5_ = bf16[256,512]{1,0:T(8,128)(2,1)S(1)} collective-permute-done((bf16[256,512]{1,0:T(8,128)(2,1)S(1)}, bf16[256,512]{1,0:T(8,128)(2,1)S(1)}, u32[]{:S(2)}, u32[]{:S(2)}) %collective-permute-start.3) | collective-permute-done | bytes 262176 | tf_op jit(solution)/shard_map/ppermute | solution.py:484
  55.4 2.7 %collective-permute-start.6 = (bf16[256,512]{1,0:T(8,128)(2,1)S(1)}, bf16[256,512]{1,0:T(8,128)(2,1)S(1)}, u32[]{:S(2)}, u32[]{:S(2)}) collective-permute-start(bf16[256,512]{1,0:T(8,128)(2,1)S(1)} %collective-permute-done.5.refs_6_), channel_id=1, source_target_pairs={{0,112},{16,0},{32,16},{48,32},{64,48},{80,64},{96,80},{112,96},{1... | collective-permute-start | bytes 786440 | tf_op jit(solution)/shard_map/ppermute | solution.py:490
  58.6 2.5 %collective-permute-start = (bf16[256,256]{1,0:T(8,128)(2,1)S(1)}, bf16[256,256]{1,0:T(8,128)(2,1)S(1)}, u32[]{:S(2)}, u32[]{:S(2)}) collective-permute-start(bf16[256,256]{1,0:T(8,128)(2,1)S(1)} %convolution_convert_fusion.3.refs_0_), channel_id=1, source_target_pairs={{0,128},{8,136},{128,0},{136,8},{1,129},{9,137},{129,1},{137,9},{2... | collective-permute-start | bytes 393224 | tf_op jit(solution)/shard_map/ppermute | solution.py:487
  61.1 3.8 %collective-permute-start.1 = (bf16[256,256]{1,0:T(8,128)(2,1)S(1)}, bf16[256,256]{1,0:T(8,128)(2,1)S(1)}, u32[]{:S(2)}, u32[]{:S(2)}) collective-permute-start(bf16[256,256]{1,0:T(8,128)(2,1)S(1)} %convolution_convert_fusion.3.refs_0_), channel_id=1, source_target_pairs={{0,136},{8,128},{128,8},{136,0},{1,137},{9,129},{129,9},{137,1},{2... | collective-permute-start | bytes 393224 | tf_op jit(solution)/shard_map/ppermute | solution.py:487
  64.9 5.0 %collective-permute-done.1.refs_2_ = bf16[256,256]{1,0:T(8,128)(2,1)S(1)} collective-permute-done((bf16[256,256]{1,0:T(8,128)(2,1)S(1)}, bf16[256,256]{1,0:T(8,128)(2,1)S(1)}, u32[]{:S(2)}, u32[]{:S(2)}) %collective-permute-start.1) | collective-permute-done | bytes 131104 | tf_op jit(solution)/shard_map/ppermute | solution.py:487
  69.9 2.6 %flash_step.3 = (f32[8,1024]{1,0:T(8,128)S(1)}, f32[256,1024]{1,0:T(8,128)S(1)}) custom-call(bf16[256,256]{1,0:T(8,128)(2,1)S(1)} %convolution_convert_fusion.3.refs_0_, bf16[256,256]{1,0:T(8,128)(2,1)S(1)} %collective-permute-done.refs_1_, bf16[256,256]{1,0:T(8,128)(2,1)S(1)} %collective-permute-done.1.refs_2_, ...), custom_call_target="tpu_custom_call" | custom-call | tf_op jit(solution)/shard_map/flash_step/pallas_call | solution.py:182
  72.6 2.7 %collective-permute-start.8 = (bf16[256,512]{1,0:T(8,128)(2,1)S(1)}, bf16[256,512]{1,0:T(8,128)(2,1)S(1)}, u32[]{:S(2)}, u32[]{:S(2)}) collective-permute-start(bf16[256,512]{1,0:T(8,128)(2,1)S(1)} %collective-permute-done.6.refs_5_), channel_id=1, source_target_pairs={{0,112},{16,0},{32,16},{48,32},{64,48},{80,64},{96,80},{112,96},{1... | collective-permute-start | bytes 786440 | tf_op jit(solution)/shard_map/ppermute | solution.py:498
  75.3 2.0 %flash_step.4 = (f32[8,1024]{1,0:T(8,128)S(1)}, f32[256,1024]{1,0:T(8,128)S(1)}) custom-call(bf16[256,256]{1,0:T(8,128)(2,1)S(1)} %convolution_convert_fusion.3.refs_0_, bf16[256,256]{1,0:T(8,128)(2,1)S(1)} %collective-permute-done.refs_1_, bf16[256,256]{1,0:T(8,128)(2,1)S(1)} %collective-permute-done.1.refs_2_, ...), custom_call_target="tpu_custom_call" | custom-call | tf_op jit(solution)/shard_map/flash_step/pallas_call | solution.py:182
  77.2 3.3 %collective-permute-done.7.refs_4_ = bf16[256,512]{1,0:T(8,128)(2,1)S(1)} collective-permute-done((bf16[256,512]{1,0:T(8,128)(2,1)S(1)}, bf16[256,512]{1,0:T(8,128)(2,1)S(1)}, u32[]{:S(2)}, u32[]{:S(2)}) %collective-permute-start.7) | collective-permute-done | bytes 262176 | tf_op jit(solution)/shard_map/ppermute | solution.py:497
  80.5 2.5 %collective-permute-start.10 = (bf16[128,512]{1,0:T(8,128)(2,1)S(1)}, bf16[128,512]{1,0:T(8,128)(2,1)S(1)}, u32[]{:S(2)}, u32[]{:S(2)}) collective-permute-start(bf16[128,512]{1,0:T(8,128)(2,1)S(1)} %slice.15), channel_id=1, source_target_pairs={{0,112},{16,0},{32,16},{48,32},{64,48},{80,64},{96,80},{112,96},{1... | collective-permute-start | bytes 393224 | tf_op jit(solution)/shard_map/ppermute | solution.py:498
  83.1 2.0 %flash_step.5 = (f32[8,1024]{1,0:T(8,128)S(1)}, f32[256,1024]{1,0:T(8,128)S(1)}) custom-call(bf16[256,256]{1,0:T(8,128)(2,1)S(1)} %convolution_convert_fusion.3.refs_0_, bf16[256,256]{1,0:T(8,128)(2,1)S(1)} %collective-permute-done.refs_1_, bf16[256,256]{1,0:T(8,128)(2,1)S(1)} %collective-permute-done.1.refs_2_, ...), custom_call_target="tpu_custom_call" | custom-call | tf_op jit(solution)/shard_map/flash_step/pallas_call | solution.py:182
  85.1 3.0 %collective-permute-done.9.refs_4_ = bf16[128,512]{1,0:T(8,128)(2,1)S(1)} collective-permute-done((bf16[128,512]{1,0:T(8,128)(2,1)S(1)}, bf16[128,512]{1,0:T(8,128)(2,1)S(1)}, u32[]{:S(2)}, u32[]{:S(2)}) %collective-permute-start.9) | collective-permute-done | bytes 131104 | tf_op jit(solution)/shard_map/ppermute | solution.py:497
  89.4 4.9 %collective-permute-start.11 = (bf16[272,256]{1,0:T(8,128)(2,1)S(1)}, bf16[272,256]{1,0:T(8,128)(2,1)S(1)}, u32[]{:S(2)}, u32[]{:S(2)}) collective-permute-start(bf16[272,256]{1,0:T(8,128)(2,1)S(1)} %get-tuple-element.80), channel_id=1, source_target_pairs={{0,128},{8,136},{128,0},{136,8},{1,129},{9,137},{129,1},{137,9},{2... | collective-permute-start | bytes 417800 | tf_op jit(solution)/shard_map/ppermute | solution.py:510
  94.4 2.0 %collective-permute-start.12 = (bf16[272,256]{1,0:T(8,128)(2,1)S(1)}, bf16[272,256]{1,0:T(8,128)(2,1)S(1)}, u32[]{:S(2)}, u32[]{:S(2)}) collective-permute-start(bf16[272,256]{1,0:T(8,128)(2,1)S(1)} %get-tuple-element.81), channel_id=1, source_target_pairs={{0,136},{8,128},{128,8},{136,0},{1,137},{9,129},{129,9},{137,1},{2... | collective-permute-start | bytes 417800 | tf_op jit(solution)/shard_map/ppermute | solution.py:510
  96.4 3.5 %residual_up.1.base = f32[32,1024]{1,0:T(8,128)S(1)} custom-call(bf16[32,2048]{1,0:T(8,128)(2,1)S(1)} %get-tuple-element.77.slab, bf16[2048,1024]{1,0:T(8,128)(2,1)} %weights.1), custom_call_target="tpu_custom_call" | custom-call | tf_op jit(solution)/shard_map/residual_up/pallas_call | solution.py:68
  102.5 4.3 %all-to-all-start.2 = ((bf16[8,2,144,128]{3,2,1,0:T(8,128)(2,1)}), bf16[8,2,144,128]{3,2,1,0:T(8,128)(2,1)S(1)}, u32[]{:S(2)}, u32[]{:S(2)}) async-start(bf16[8,2,144,128]{3,2,1,0:T(8,128)(2,1)} %merge_heads.1), calls=%async_computation.2 | async-start | bytes 1179648 | tf_op jit(solution)/shard_map/all_to_all | solution.py:514
  108.5 8.3 %all-to-all-done.2.pieces = bf16[8,2,144,128]{3,2,1,0:T(8,128)(2,1)S(1)} async-done(((bf16[8,2,144,128]{3,2,1,0:T(8,128)(2,1)}), bf16[8,2,144,128]{3,2,1,0:T(8,128)(2,1)S(1)}, u32[]{:S(2)}, u32[]{:S(2)}) %all-to-all-start.2) | async-done | bytes 589856 | tf_op jit(solution)/shard_map/all_to_all | solution.py:514
  117.4 1.9 %collective-permute-start.14 = (bf16[288,128]{1,0:T(8,128)(2,1)S(1)}, bf16[288,128]{1,0:T(8,128)(2,1)S(1)}, u32[]{:S(2)}, u32[]{:S(2)}) collective-permute-start(bf16[288,128]{1,0:T(8,128)(2,1)S(1)} %get-tuple-element.89), channel_id=1, source_target_pairs={{0,8},{8,0},{1,9},{9,1},{2,10},{10,2},{3,11},{11,3},{4,12},{12,4},... | collective-permute-start | bytes 221192 | tf_op jit(solution)/shard_map/ppermute | solution.py:521
  119.3 2.1 %collective-permute-start.15 = (bf16[288,128]{1,0:T(8,128)(2,1)S(1)}, bf16[288,128]{1,0:T(8,128)(2,1)S(1)}, u32[]{:S(2)}, u32[]{:S(2)}) collective-permute-start(bf16[288,128]{1,0:T(8,128)(2,1)S(1)} %get-tuple-element.90), channel_id=1, source_target_pairs={{8,16},{24,32},{40,48},{56,64},{72,80},{88,96},{104,112},{120,128}... | collective-permute-start | bytes 221192 | tf_op jit(solution)/shard_map/ppermute | solution.py:523
  121.5 3.4 %collective-permute-done.15.far_up = bf16[288,128]{1,0:T(8,128)(2,1)S(1)} collective-permute-done((bf16[288,128]{1,0:T(8,128)(2,1)S(1)}, bf16[288,128]{1,0:T(8,128)(2,1)S(1)}, u32[]{:S(2)}, u32[]{:S(2)}) %collective-permute-start.15) | collective-permute-done | bytes 73760 | tf_op jit(solution)/shard_map/ppermute | solution.py:523
  125.0 2.8 %fine_stage.1 = (bf16[4,64,128]{2,1,0:T(8,128)(2,1)}, bf16[4,64,128]{2,1,0:T(8,128)(2,1)}, bf16[768,128]{1,0:T(8,128)(2,1)S(1)}) custom-call(s32[5]{0:T(128)S(1)} %convert_element_type.28.flags, bf16[2,144,128]{2,1,0:T(8,128)(2,1)S(1)} %get-tuple-element.88.own, bf16[288,128]{1,0:T(8,128)(2,1)S(1)} %collective-permute-done.14.near_up, ...), custom_call_target="tpu_custom_call" | custom-call | tf_op jit(solution)/shard_map/fine_stage/pallas_call | solution.py:403
  127.7 8.6 %all_to_all.31 = bf16[16,48,128]{2,1,0:T(8,128)(2,1)S(1)} all-to-all(bf16[16,48,128]{2,1,0:T(8,128)(2,1)S(1)} %bitcast.52), channel_id=1, replica_groups=mesh['xh'=2,'z'=8,'core'=2,'y'=4,'xl'=2] {'core','y','xl'}, dimensions={0} | all-to-all | bytes 393216 | tf_op jit(solution)/shard_map/all_to_all | solution.py:529
  136.4 6.3 %collective-permute-start.16 = (bf16[48,128]{1,0:T(8,128)(2,1)S(1)}, bf16[48,128]{1,0:T(8,128)(2,1)S(1)}, u32[]{:S(2)}, u32[]{:S(2)}) collective-permute-start(bf16[48,128]{1,0:T(8,128)(2,1)S(1)} %reduce_sum.24), channel_id=1, source_target_pairs={{0,128},{128,0},{1,129},{129,1},{2,130},{130,2},{3,131},{131,3},{4... | collective-permute-start | bytes 36872 | tf_op jit(solution)/shard_map/ppermute | solution.py:531
  143.9 10.6 %all_to_all.32 = bf16[8,48,128]{2,1,0:T(8,128)(2,1)S(1)} all-to-all(bf16[8,48,128]{2,1,0:T(8,128)(2,1)S(1)} %broadcast_in_dim.4), channel_id=1, replica_groups=mesh['xh'=2,'z'=8,'core'=2,'y'=4,'xl'=2] {'z'}, dimensions={0} | all-to-all | bytes 196608 | tf_op jit(solution)/shard_map/all_to_all | solution.py:439
  154.5 12.4 %all_to_all.33 = bf16[16,48,128]{2,1,0:T(8,128)(2,1)S(1)} all-to-all(bf16[16,48,128]{2,1,0:T(8,128)(2,1)S(1)} %broadcast_in_dim.5), channel_id=1, replica_groups=mesh['xh'=2,'z'=8,'core'=2,'y'=4,'xl'=2] {'core','y','xl'}, dimensions={0} | all-to-all | bytes 393216 | tf_op jit(solution)/shard_map/all_to_all | solution.py:439
  (75 shorter events, 12.7 us)
Async XLA Ops:
  0.6 10.0 %copy-start = (bf16[256,2048]{1,0:T(8,128)(2,1)S(1)}, bf16[256,2048]{1,0:T(8,128)(2,1)}, u32[]{:S(2)}) copy-start(bf16[256,2048]{1,0:T(8,128)(2,1)} %param.22) | copy-start | bytes 3145732
  3.3 20.5 %all-to-all-start = ((bf16[8,32,2048]{2,1,0:T(8,128)(2,1)}), bf16[8,32,2048]{2,1,0:T(8,128)(2,1)S(1)}, u32[]{:S(2)}, u32[]{:S(2)}) async-start(bf16[8,32,2048]{2,1,0:T(8,128)(2,1)} %bitcast.9), calls=%async_computation | async-start | bytes 2097152 | tf_op jit(solution)/shard_map/all_to_all | solution.py:469
  9.2 14.6 %copy-start.4 = (f32[2048]{0:T(1024)S(1)}, f32[2048]{0:T(1024)}, u32[]{:S(2)}) copy-start(f32[2048]{0:T(1024)} %param.18) | copy-start | bytes 24580
  23.7 20.8 %copy-start.5 = (bf16[2048,256]{1,0:T(8,128)(2,1)S(1)}, bf16[2048,256]{1,0:T(8,128)(2,1)}, u32[]{:S(2)}) copy-start(bf16[2048,256]{1,0:T(8,128)(2,1)} %param.20) | copy-start | bytes 3145732
  23.7 34.4 %copy-start.6 = (bf16[2048,256]{1,0:T(8,128)(2,1)S(1)}, bf16[2048,256]{1,0:T(8,128)(2,1)}, u32[]{:S(2)}) copy-start(bf16[2048,256]{1,0:T(8,128)(2,1)} %param.19) | copy-start | bytes 3145732
  45.0 10.4 %collective-permute-start.3 = (bf16[256,512]{1,0:T(8,128)(2,1)S(1)}, bf16[256,512]{1,0:T(8,128)(2,1)S(1)}, u32[]{:S(2)}, u32[]{:S(2)}) collective-permute-start(bf16[256,512]{1,0:T(8,128)(2,1)S(1)} %pad_maximum_fusion.1.refs_4_), channel_id=1, source_target_pairs={{0,16},{16,32},{32,48},{48,64},{64,80},{80,96},{96,112},{112,0},{1... | collective-permute-start | bytes 786440 | tf_op jit(solution)/shard_map/ppermute | solution.py:484
  46.7 8.7 %collective-permute-start.5 = (bf16[256,512]{1,0:T(8,128)(2,1)S(1)}, bf16[256,512]{1,0:T(8,128)(2,1)S(1)}, u32[]{:S(2)}, u32[]{:S(2)}) collective-permute-start(bf16[256,512]{1,0:T(8,128)(2,1)S(1)} %pad_maximum_fusion.1.refs_4_), channel_id=1, source_target_pairs={{0,112},{16,0},{32,16},{48,32},{64,48},{80,64},{96,80},{112,96},{1... | collective-permute-start | bytes 786440 | tf_op jit(solution)/shard_map/ppermute | solution.py:485
  55.4 17.0 %collective-permute-start.4 = (bf16[256,512]{1,0:T(8,128)(2,1)S(1)}, bf16[256,512]{1,0:T(8,128)(2,1)S(1)}, u32[]{:S(2)}, u32[]{:S(2)}) collective-permute-start(bf16[256,512]{1,0:T(8,128)(2,1)S(1)} %collective-permute-done.3.refs_5_), channel_id=1, source_target_pairs={{0,16},{16,32},{32,48},{48,64},{64,80},{80,96},{96,112},{112,0},{1... | collective-permute-start | bytes 786440 | tf_op jit(solution)/shard_map/ppermute | solution.py:489
  55.4 17.0 %collective-permute-start.6 = (bf16[256,512]{1,0:T(8,128)(2,1)S(1)}, bf16[256,512]{1,0:T(8,128)(2,1)S(1)}, u32[]{:S(2)}, u32[]{:S(2)}) collective-permute-start(bf16[256,512]{1,0:T(8,128)(2,1)S(1)} %collective-permute-done.5.refs_6_), channel_id=1, source_target_pairs={{0,112},{16,0},{32,16},{48,32},{64,48},{80,64},{96,80},{112,96},{1... | collective-permute-start | bytes 786440 | tf_op jit(solution)/shard_map/ppermute | solution.py:490
  58.6 6.3 %collective-permute-start = (bf16[256,256]{1,0:T(8,128)(2,1)S(1)}, bf16[256,256]{1,0:T(8,128)(2,1)S(1)}, u32[]{:S(2)}, u32[]{:S(2)}) collective-permute-start(bf16[256,256]{1,0:T(8,128)(2,1)S(1)} %convolution_convert_fusion.3.refs_0_), channel_id=1, source_target_pairs={{0,128},{8,136},{128,0},{136,8},{1,129},{9,137},{129,1},{137,9},{2... | collective-permute-start | bytes 393224 | tf_op jit(solution)/shard_map/ppermute | solution.py:487
  61.1 8.7 %collective-permute-start.1 = (bf16[256,256]{1,0:T(8,128)(2,1)S(1)}, bf16[256,256]{1,0:T(8,128)(2,1)S(1)}, u32[]{:S(2)}, u32[]{:S(2)}) collective-permute-start(bf16[256,256]{1,0:T(8,128)(2,1)S(1)} %convolution_convert_fusion.3.refs_0_), channel_id=1, source_target_pairs={{0,136},{8,128},{128,8},{136,0},{1,137},{9,129},{129,9},{137,1},{2... | collective-permute-start | bytes 393224 | tf_op jit(solution)/shard_map/ppermute | solution.py:487
  64.9 5.0 %collective-permute-start.2 = (bf16[256,256]{1,0:T(8,128)(2,1)S(1)}, bf16[256,256]{1,0:T(8,128)(2,1)S(1)}, u32[]{:S(2)}, u32[]{:S(2)}) collective-permute-start(bf16[256,256]{1,0:T(8,128)(2,1)S(1)} %convolution_convert_fusion.3.refs_0_), channel_id=1, source_target_pairs={{0,8},{8,0},{128,136},{136,128},{1,9},{9,1},{129,137},{137,129},{2... | collective-permute-start | bytes 393224 | tf_op jit(solution)/shard_map/ppermute | solution.py:487
  72.5 8.0 %collective-permute-start.7 = (bf16[256,512]{1,0:T(8,128)(2,1)S(1)}, bf16[256,512]{1,0:T(8,128)(2,1)S(1)}, u32[]{:S(2)}, u32[]{:S(2)}) collective-permute-start(bf16[256,512]{1,0:T(8,128)(2,1)S(1)} %collective-permute-done.4.refs_4_), channel_id=1, source_target_pairs={{0,16},{16,32},{32,48},{48,64},{64,80},{80,96},{96,112},{112,0},{1... | collective-permute-start | bytes 786440 | tf_op jit(solution)/shard_map/ppermute | solution.py:497
  72.6 7.9 %collective-permute-start.8 = (bf16[256,512]{1,0:T(8,128)(2,1)S(1)}, bf16[256,512]{1,0:T(8,128)(2,1)S(1)}, u32[]{:S(2)}, u32[]{:S(2)}) collective-permute-start(bf16[256,512]{1,0:T(8,128)(2,1)S(1)} %collective-permute-done.6.refs_5_), channel_id=1, source_target_pairs={{0,112},{16,0},{32,16},{48,32},{64,48},{80,64},{96,80},{112,96},{1... | collective-permute-start | bytes 786440 | tf_op jit(solution)/shard_map/ppermute | solution.py:498
  80.5 4.6 %collective-permute-start.10 = (bf16[128,512]{1,0:T(8,128)(2,1)S(1)}, bf16[128,512]{1,0:T(8,128)(2,1)S(1)}, u32[]{:S(2)}, u32[]{:S(2)}) collective-permute-start(bf16[128,512]{1,0:T(8,128)(2,1)S(1)} %slice.15), channel_id=1, source_target_pairs={{0,112},{16,0},{32,16},{48,32},{64,48},{80,64},{96,80},{112,96},{1... | collective-permute-start | bytes 393224 | tf_op jit(solution)/shard_map/ppermute | solution.py:498
  83.0 5.1 %collective-permute-start.9 = (bf16[128,512]{1,0:T(8,128)(2,1)S(1)}, bf16[128,512]{1,0:T(8,128)(2,1)S(1)}, u32[]{:S(2)}, u32[]{:S(2)}) collective-permute-start(bf16[128,512]{1,0:T(8,128)(2,1)S(1)} %slice.14), channel_id=1, source_target_pairs={{0,16},{16,32},{32,48},{48,64},{64,80},{80,96},{96,112},{112,0},{1... | collective-permute-start | bytes 393224 | tf_op jit(solution)/shard_map/ppermute | solution.py:497
  89.4 17.6 %copy-start.8 = (bf16[9,64,64]{2,1,0:T(8,128)(2,1)S(1)}, bf16[9,64,64]{2,1,0:T(8,128)(2,1)}, u32[]{:S(2)}) copy-start(bf16[9,64,64]{2,1,0:T(8,128)(2,1)} %param.26) | copy-start | bytes 221188
  89.4 10.6 %collective-permute-start.11 = (bf16[272,256]{1,0:T(8,128)(2,1)S(1)}, bf16[272,256]{1,0:T(8,128)(2,1)S(1)}, u32[]{:S(2)}, u32[]{:S(2)}) collective-permute-start(bf16[272,256]{1,0:T(8,128)(2,1)S(1)} %get-tuple-element.80), channel_id=1, source_target_pairs={{0,128},{8,136},{128,0},{136,8},{1,129},{9,137},{129,1},{137,9},{2... | collective-permute-start | bytes 417800 | tf_op jit(solution)/shard_map/ppermute | solution.py:510
  94.4 6.9 %collective-permute-start.12 = (bf16[272,256]{1,0:T(8,128)(2,1)S(1)}, bf16[272,256]{1,0:T(8,128)(2,1)S(1)}, u32[]{:S(2)}, u32[]{:S(2)}) collective-permute-start(bf16[272,256]{1,0:T(8,128)(2,1)S(1)} %get-tuple-element.81), channel_id=1, source_target_pairs={{0,136},{8,128},{128,8},{136,0},{1,137},{9,129},{129,9},{137,1},{2... | collective-permute-start | bytes 417800 | tf_op jit(solution)/shard_map/ppermute | solution.py:510
  96.4 4.9 %collective-permute-start.13 = (bf16[272,256]{1,0:T(8,128)(2,1)S(1)}, bf16[272,256]{1,0:T(8,128)(2,1)S(1)}, u32[]{:S(2)}, u32[]{:S(2)}) collective-permute-start(bf16[272,256]{1,0:T(8,128)(2,1)S(1)} %get-tuple-element.82), channel_id=1, source_target_pairs={{0,8},{8,0},{128,136},{136,128},{1,9},{9,1},{129,137},{137,129},{2... | collective-permute-start | bytes 417800 | tf_op jit(solution)/shard_map/ppermute | solution.py:510
  96.4 11.0 %copy-start.7 = (bf16[9,64,64]{2,1,0:T(8,128)(2,1)S(1)}, bf16[9,64,64]{2,1,0:T(8,128)(2,1)}, u32[]{:S(2)}) copy-start(bf16[9,64,64]{2,1,0:T(8,128)(2,1)} %param.24) | copy-start | bytes 221188
  99.9 16.8 %copy-start.1 = (bf16[4,64,128]{2,1,0:T(8,128)(2,1)S(1)}, bf16[4,64,128]{2,1,0:T(8,128)(2,1)}, u32[]{:S(2)}) copy-start(bf16[4,64,128]{2,1,0:T(8,128)(2,1)} %grad.1) | copy-start | bytes 196612
  99.9 21.5 %copy-start.9 = (f32[64]{0:T(128)S(1)}, f32[64]{0:T(128)}, u32[]{:S(2)}) copy-start(f32[64]{0:T(128)} %param.25) | copy-start | bytes 772
  100.0 25.0 %copy-start.2 = (bf16[144,1024]{1,0:T(8,128)(2,1)S(1)}, bf16[144,1024]{1,0:T(8,128)(2,1)}, u32[]{:S(2)}) copy-start(bf16[144,1024]{1,0:T(8,128)(2,1)} %constant.37.clone.spread) | copy-start | bytes 884740
  100.0 25.0 %copy-start.3 = (bf16[32,1024]{1,0:T(8,128)(2,1)S(1)}, bf16[32,1024]{1,0:T(8,128)(2,1)}, u32[]{:S(2)}) copy-start(bf16[32,1024]{1,0:T(8,128)(2,1)} %constant.38.clone.edges) | copy-start | bytes 196612
  102.5 14.2 %all-to-all-start.2 = ((bf16[8,2,144,128]{3,2,1,0:T(8,128)(2,1)}), bf16[8,2,144,128]{3,2,1,0:T(8,128)(2,1)S(1)}, u32[]{:S(2)}, u32[]{:S(2)}) async-start(bf16[8,2,144,128]{3,2,1,0:T(8,128)(2,1)} %merge_heads.1), calls=%async_computation.2 | async-start | bytes 1179648 | tf_op jit(solution)/shard_map/all_to_all | solution.py:514
  117.4 4.2 %collective-permute-start.14 = (bf16[288,128]{1,0:T(8,128)(2,1)S(1)}, bf16[288,128]{1,0:T(8,128)(2,1)S(1)}, u32[]{:S(2)}, u32[]{:S(2)}) collective-permute-start(bf16[288,128]{1,0:T(8,128)(2,1)S(1)} %get-tuple-element.89), channel_id=1, source_target_pairs={{0,8},{8,0},{1,9},{9,1},{2,10},{10,2},{3,11},{11,3},{4,12},{12,4},... | collective-permute-start | bytes 221192 | tf_op jit(solution)/shard_map/ppermute | solution.py:521
  119.3 5.7 %collective-permute-start.15 = (bf16[288,128]{1,0:T(8,128)(2,1)S(1)}, bf16[288,128]{1,0:T(8,128)(2,1)S(1)}, u32[]{:S(2)}, u32[]{:S(2)}) collective-permute-start(bf16[288,128]{1,0:T(8,128)(2,1)S(1)} %get-tuple-element.90), channel_id=1, source_target_pairs={{8,16},{24,32},{40,48},{56,64},{72,80},{88,96},{104,112},{120,128}... | collective-permute-start | bytes 221192 | tf_op jit(solution)/shard_map/ppermute | solution.py:523
  136.4 7.4 %collective-permute-start.16 = (bf16[48,128]{1,0:T(8,128)(2,1)S(1)}, bf16[48,128]{1,0:T(8,128)(2,1)S(1)}, u32[]{:S(2)}, u32[]{:S(2)}) collective-permute-start(bf16[48,128]{1,0:T(8,128)(2,1)S(1)} %reduce_sum.24), channel_id=1, source_target_pairs={{0,128},{128,0},{1,129},{129,1},{2,130},{130,2},{3,131},{131,3},{4... | collective-permute-start | bytes 36872 | tf_op jit(solution)/shard_map/ppermute | solution.py:531
where the time goes:
time: 168 us
  blocking collectives  50.5 us (30%)
  starting transfers between devices  47.7 us (28%)
  waiting for transfers between devices  39.6 us (24%)
  Pallas kernels  19.8 us (12%)
  matrix products  5.98 us (4%)
  local copies, waits for them, and re-layouts  3.08 us (2%)
    all_to_all x2, blocking collectives, copies(): lax.all_to_all(jnp.broadcast_to(piece[None], (count,) + piece.shape), axi...  23 us
    all_to_all x1, blocking collectives, device_step(): normed = lax.all_to_all(spread_out, VAR, 0, 0).reshape(256, D)  18.9 us
    all_to_all x1, waiting for transfers between devices, device_step(): pieces = lax.all_to_all(partial_mix, VAR, 0, 0)  9.67 us
    all_to_all x1, blocking collectives, device_step(): shares = lax.all_to_all(terms.reshape(16, 48, 128), BOARD, 0, 0)  8.65 us
    all_to_all x1, waiting for transfers between devices, device_step(): pieces = lax.all_to_all(merged, VAR, 0, 0)  8.25 us
    pallas_call x4, Pallas kernels, flash_step(): pl.pallas_call(flash_kernel(blocks, len(chunks), first, last), out_shape=...  7.87 us
    ppermute x3, starting transfers between devices, device_step(): behind = lax.ppermute(behind, 'z', turn(8, -1))  7.81 us
    ppermute x3, starting transfers between devices, device_step(): lax.ppermute(b, group, flip(4, k))  7 us
  transfers between devices with their start and end apart: 19, of which 9 were waited for; matrix products, arithmetic and copies ran while one was open for 4% of the time, Pallas kernels for 6%

commit v1 on v0

--- a/solution.py
+++ b/solution.py
@@ -14,7 +14,7 @@
 C = 64
 BAND = ("xh", "z", "core")
 VAR = ("y", "xl")
-BOARD = ("core", "y", "xl")
+PLANE = ("xh", "core", "y", "xl")
 BF = jnp.bfloat16
 F32 = jnp.float32
 VMEM_SPEC = pl.BlockSpec(memory_space=pltpu.VMEM)
@@ -526,12 +526,10 @@
     field_out, grad_fine, terms = fine_stage(
         flags, up, near_up, far_up, spread, jnp.asarray(edge_matrix(), BF), cells, mats, bias, factor
     )
-    shares = lax.all_to_all(terms.reshape(16, 48, 128), BOARD, 0, 0)
+    shares = lax.all_to_all(terms.reshape(32, 24, 128), PLANE, 0, 0)
     share = jnp.sum(shares.astype(F32), axis=0).astype(BF)
-    other = lax.ppermute(share, "xh", flip(2, 1))
-    share = (share.astype(F32) + other.astype(F32)).astype(BF)
     share = jnp.sum(copies(share, "z", 8).astype(F32), axis=0).astype(BF)
-    totals = copies(share, BOARD, 16).reshape(768, 128)
+    totals = copies(share, PLANE, 32).reshape(768, 128)
     first, second, third = finish(totals)
     return (field_out, grad_fine, first.reshape(9, C, C), second.reshape(9, C, C), third.reshape(C))
 

time: 168 us -> 169 us (level)
  blocking collectives: 50.5 us -> 58.7 us
  starting transfers between devices: 47.7 us -> 41.3 us
    all_to_all x1, blocking collectives: 8.65 us -> 16.6 us  [device_step(): shares = lax.all_to_all(terms.reshape(32, 24, 128), PLANE, 0, 0)]
    ppermute x1 -> x0, starting transfers between devices: 6.34 us -> none  [device_step(): other = lax.ppermute(share, 'xh', flip(2, 1))]
  transfers between devices with their start and end apart: 19 -> 18, of which waited for: 9 -> 8; matrix products, arithmetic and copies ran while one was open for 4% -> 4% of each run, Pallas kernels for 6% -> 6%
where the time goes in v1:
time: 169 us
  blocking collectives  58.7 us (35%)
  starting transfers between devices  41.3 us (24%)
  waiting for transfers between devices  38.5 us (23%)
  Pallas kernels  19.8 us (12%)
  matrix products  5.98 us (4%)
  local copies, waits for them, and re-layouts  3.07 us (2%)
    all_to_all x2, blocking collectives, copies(): lax.all_to_all(jnp.broadcast_to(piece[None], (count,) + piece.shape), axi...  23.3 us
    all_to_all x1, blocking collectives, device_step(): normed = lax.all_to_all(spread_out, VAR, 0, 0).reshape(256, D)  18.9 us
    all_to_all x1, blocking collectives, device_step(): shares = lax.all_to_all(terms.reshape(32, 24, 128), PLANE, 0, 0)  16.6 us
    all_to_all x1, waiting for transfers between devices, device_step(): pieces = lax.all_to_all(partial_mix, VAR, 0, 0)  9.67 us
    all_to_all x1, waiting for transfers between devices, device_step(): pieces = lax.all_to_all(merged, VAR, 0, 0)  8.25 us
    pallas_call x4, Pallas kernels, flash_step(): pl.pallas_call(flash_kernel(blocks, len(chunks), first, last), out_shape=...  7.87 us
    ppermute x3, starting transfers between devices, device_step(): behind = lax.ppermute(behind, 'z', turn(8, -1))  7.81 us
    ppermute x3, starting transfers between devices, device_step(): lax.ppermute(b, group, flip(4, k))  7 us
  transfers between devices with their start and end apart: 18, of which 8 were waited for; matrix products, arithmetic and copies ran while one was open for 4% of the time, Pallas kernels for 6%

profile of v1, /device:TPU:1, one launch (start us, length us, event | category | flops | bytes accessed | tf_op | source)
XLA Modules:
  0.0 168.5 jit_solution(872529139313310904)
XLA Ops:
  0.6 2.6 %mix_variables.1 = bf16[256,2048]{1,0:T(8,128)(2,1)} custom-call(bf16[128,256]{1,0:T(8,128)(2,1)} %bitcast.66, bf16[128,2048]{1,0:T(8,128)(2,1)} %bitcast.65, f32[2,2048]{1,0:T(2,128)} %offsets.1), custom_call_target="tpu_custom_call" | custom-call | tf_op jit(solution)/shard_map/mix_variables/pallas_call | solution.py:48
  3.2 5.9 %all-to-all-start = ((bf16[8,32,2048]{2,1,0:T(8,128)(2,1)}), bf16[8,32,2048]{2,1,0:T(8,128)(2,1)S(1)}, u32[]{:S(2)}, u32[]{:S(2)}) async-start(bf16[8,32,2048]{2,1,0:T(8,128)(2,1)} %bitcast.9), calls=%async_computation | async-start | bytes 2097152 | tf_op jit(solution)/shard_map/all_to_all | solution.py:469
  10.6 3.4 %convolution_convert_fusion.mat = bf16[256,1024]{1,0:T(8,128)(2,1)S(1)} fusion(bf16[256,2048]{1,0:T(8,128)(2,1)S(1)} %copy-done, bf16[2048,1024]{1,0:T(8,128)(2,1)} %weights.1), kind=kOutput, calls=%fused_computation | convolution fusion | flops 1074003968 | bytes 5767168 | tf_op jit(solution)/shard_map/dot_general | solution.py:470
  14.0 9.7 %all-to-all-done.pieces = bf16[8,32,2048]{2,1,0:T(8,128)(2,1)S(1)} async-done(((bf16[8,32,2048]{2,1,0:T(8,128)(2,1)}), bf16[8,32,2048]{2,1,0:T(8,128)(2,1)S(1)}, u32[]{:S(2)}, u32[]{:S(2)}) %all-to-all-start) | async-done | bytes 1048608 | tf_op jit(solution)/shard_map/all_to_all | solution.py:469
  24.0 18.9 %all_to_all.30 = bf16[8,32,2048]{2,1,0:T(8,128)(2,1)S(1)} all-to-all(bf16[8,32,2048]{2,1,0:T(8,128)(2,1)S(1)} %get-tuple-element.56), channel_id=1, replica_groups=mesh['xh'=2,'z'=8,'core'=2,'y'=4,'xl'=2] {'y','xl'}, dimensions={0} | all-to-all | bytes 2097152 | tf_op jit(solution)/shard_map/all_to_all | solution.py:479
  42.8 1.7 convolution_convert_fusion.1
  45.0 1.7 %collective-permute-start.3 = (bf16[256,512]{1,0:T(8,128)(2,1)S(1)}, bf16[256,512]{1,0:T(8,128)(2,1)S(1)}, u32[]{:S(2)}, u32[]{:S(2)}) collective-permute-start(bf16[256,512]{1,0:T(8,128)(2,1)S(1)} %pad_maximum_fusion.1.refs_4_), channel_id=1, source_target_pairs={{0,16},{16,32},{32,48},{48,64},{64,80},{80,96},{96,112},{112,0},{1... | collective-permute-start | bytes 786440 | tf_op jit(solution)/shard_map/ppermute | solution.py:484
  46.7 4.0 %collective-permute-start.5 = (bf16[256,512]{1,0:T(8,128)(2,1)S(1)}, bf16[256,512]{1,0:T(8,128)(2,1)S(1)}, u32[]{:S(2)}, u32[]{:S(2)}) collective-permute-start(bf16[256,512]{1,0:T(8,128)(2,1)S(1)} %pad_maximum_fusion.1.refs_4_), channel_id=1, source_target_pairs={{0,112},{16,0},{32,16},{48,32},{64,48},{80,64},{96,80},{112,96},{1... | collective-permute-start | bytes 786440 | tf_op jit(solution)/shard_map/ppermute | solution.py:485
  50.7 4.7 %collective-permute-done.3.refs_5_ = bf16[256,512]{1,0:T(8,128)(2,1)S(1)} collective-permute-done((bf16[256,512]{1,0:T(8,128)(2,1)S(1)}, bf16[256,512]{1,0:T(8,128)(2,1)S(1)}, u32[]{:S(2)}, u32[]{:S(2)}) %collective-permute-start.3) | collective-permute-done | bytes 262176 | tf_op jit(solution)/shard_map/ppermute | solution.py:484
  55.4 2.7 %collective-permute-start.6 = (bf16[256,512]{1,0:T(8,128)(2,1)S(1)}, bf16[256,512]{1,0:T(8,128)(2,1)S(1)}, u32[]{:S(2)}, u32[]{:S(2)}) collective-permute-start(bf16[256,512]{1,0:T(8,128)(2,1)S(1)} %collective-permute-done.5.refs_6_), channel_id=1, source_target_pairs={{0,112},{16,0},{32,16},{48,32},{64,48},{80,64},{96,80},{112,96},{1... | collective-permute-start | bytes 786440 | tf_op jit(solution)/shard_map/ppermute | solution.py:490
  58.5 2.5 %collective-permute-start = (bf16[256,256]{1,0:T(8,128)(2,1)S(1)}, bf16[256,256]{1,0:T(8,128)(2,1)S(1)}, u32[]{:S(2)}, u32[]{:S(2)}) collective-permute-start(bf16[256,256]{1,0:T(8,128)(2,1)S(1)} %convolution_convert_fusion.3.refs_0_), channel_id=1, source_target_pairs={{0,128},{8,136},{128,0},{136,8},{1,129},{9,137},{129,1},{137,9},{2... | collective-permute-start | bytes 393224 | tf_op jit(solution)/shard_map/ppermute | solution.py:487
  61.1 3.7 %collective-permute-start.1 = (bf16[256,256]{1,0:T(8,128)(2,1)S(1)}, bf16[256,256]{1,0:T(8,128)(2,1)S(1)}, u32[]{:S(2)}, u32[]{:S(2)}) collective-permute-start(bf16[256,256]{1,0:T(8,128)(2,1)S(1)} %convolution_convert_fusion.3.refs_0_), channel_id=1, source_target_pairs={{0,136},{8,128},{128,8},{136,0},{1,137},{9,129},{129,9},{137,1},{2... | collective-permute-start | bytes 393224 | tf_op jit(solution)/shard_map/ppermute | solution.py:487
  64.8 5.0 %collective-permute-done.1.refs_2_ = bf16[256,256]{1,0:T(8,128)(2,1)S(1)} collective-permute-done((bf16[256,256]{1,0:T(8,128)(2,1)S(1)}, bf16[256,256]{1,0:T(8,128)(2,1)S(1)}, u32[]{:S(2)}, u32[]{:S(2)}) %collective-permute-start.1) | collective-permute-done | bytes 131104 | tf_op jit(solution)/shard_map/ppermute | solution.py:487
  69.8 2.6 %flash_step.3 = (f32[8,1024]{1,0:T(8,128)S(1)}, f32[256,1024]{1,0:T(8,128)S(1)}) custom-call(bf16[256,256]{1,0:T(8,128)(2,1)S(1)} %convolution_convert_fusion.3.refs_0_, bf16[256,256]{1,0:T(8,128)(2,1)S(1)} %collective-permute-done.refs_1_, bf16[256,256]{1,0:T(8,128)(2,1)S(1)} %collective-permute-done.1.refs_2_, ...), custom_call_target="tpu_custom_call" | custom-call | tf_op jit(solution)/shard_map/flash_step/pallas_call | solution.py:182
  72.6 2.7 %collective-permute-start.8 = (bf16[256,512]{1,0:T(8,128)(2,1)S(1)}, bf16[256,512]{1,0:T(8,128)(2,1)S(1)}, u32[]{:S(2)}, u32[]{:S(2)}) collective-permute-start(bf16[256,512]{1,0:T(8,128)(2,1)S(1)} %collective-permute-done.6.refs_5_), channel_id=1, source_target_pairs={{0,112},{16,0},{32,16},{48,32},{64,48},{80,64},{96,80},{112,96},{1... | collective-permute-start | bytes 786440 | tf_op jit(solution)/shard_map/ppermute | solution.py:498
  75.2 2.0 %flash_step.4 = (f32[8,1024]{1,0:T(8,128)S(1)}, f32[256,1024]{1,0:T(8,128)S(1)}) custom-call(bf16[256,256]{1,0:T(8,128)(2,1)S(1)} %convolution_convert_fusion.3.refs_0_, bf16[256,256]{1,0:T(8,128)(2,1)S(1)} %collective-permute-done.refs_1_, bf16[256,256]{1,0:T(8,128)(2,1)S(1)} %collective-permute-done.1.refs_2_, ...), custom_call_target="tpu_custom_call" | custom-call | tf_op jit(solution)/shard_map/flash_step/pallas_call | solution.py:182
  77.2 3.3 %collective-permute-done.7.refs_4_ = bf16[256,512]{1,0:T(8,128)(2,1)S(1)} collective-permute-done((bf16[256,512]{1,0:T(8,128)(2,1)S(1)}, bf16[256,512]{1,0:T(8,128)(2,1)S(1)}, u32[]{:S(2)}, u32[]{:S(2)}) %collective-permute-start.7) | collective-permute-done | bytes 262176 | tf_op jit(solution)/shard_map/ppermute | solution.py:497
  80.5 2.5 %collective-permute-start.10 = (bf16[128,512]{1,0:T(8,128)(2,1)S(1)}, bf16[128,512]{1,0:T(8,128)(2,1)S(1)}, u32[]{:S(2)}, u32[]{:S(2)}) collective-permute-start(bf16[128,512]{1,0:T(8,128)(2,1)S(1)} %slice.15), channel_id=1, source_target_pairs={{0,112},{16,0},{32,16},{48,32},{64,48},{80,64},{96,80},{112,96},{1... | collective-permute-start | bytes 393224 | tf_op jit(solution)/shard_map/ppermute | solution.py:498
  83.1 2.0 %flash_step.5 = (f32[8,1024]{1,0:T(8,128)S(1)}, f32[256,1024]{1,0:T(8,128)S(1)}) custom-call(bf16[256,256]{1,0:T(8,128)(2,1)S(1)} %convolution_convert_fusion.3.refs_0_, bf16[256,256]{1,0:T(8,128)(2,1)S(1)} %collective-permute-done.refs_1_, bf16[256,256]{1,0:T(8,128)(2,1)S(1)} %collective-permute-done.1.refs_2_, ...), custom_call_target="tpu_custom_call" | custom-call | tf_op jit(solution)/shard_map/flash_step/pallas_call | solution.py:182
  85.1 3.0 %collective-permute-done.9.refs_4_ = bf16[128,512]{1,0:T(8,128)(2,1)S(1)} collective-permute-done((bf16[128,512]{1,0:T(8,128)(2,1)S(1)}, bf16[128,512]{1,0:T(8,128)(2,1)S(1)}, u32[]{:S(2)}, u32[]{:S(2)}) %collective-permute-start.9) | collective-permute-done | bytes 131104 | tf_op jit(solution)/shard_map/ppermute | solution.py:497
  89.4 4.9 %collective-permute-start.11 = (bf16[272,256]{1,0:T(8,128)(2,1)S(1)}, bf16[272,256]{1,0:T(8,128)(2,1)S(1)}, u32[]{:S(2)}, u32[]{:S(2)}) collective-permute-start(bf16[272,256]{1,0:T(8,128)(2,1)S(1)} %get-tuple-element.80), channel_id=1, source_target_pairs={{0,128},{8,136},{128,0},{136,8},{1,129},{9,137},{129,1},{137,9},{2... | collective-permute-start | bytes 417800 | tf_op jit(solution)/shard_map/ppermute | solution.py:510
  94.3 2.0 %collective-permute-start.12 = (bf16[272,256]{1,0:T(8,128)(2,1)S(1)}, bf16[272,256]{1,0:T(8,128)(2,1)S(1)}, u32[]{:S(2)}, u32[]{:S(2)}) collective-permute-start(bf16[272,256]{1,0:T(8,128)(2,1)S(1)} %get-tuple-element.81), channel_id=1, source_target_pairs={{0,136},{8,128},{128,8},{136,0},{1,137},{9,129},{129,9},{137,1},{2... | collective-permute-start | bytes 417800 | tf_op jit(solution)/shard_map/ppermute | solution.py:510
  96.4 3.5 %residual_up.1.base = f32[32,1024]{1,0:T(8,128)S(1)} custom-call(bf16[32,2048]{1,0:T(8,128)(2,1)S(1)} %get-tuple-element.77.slab, bf16[2048,1024]{1,0:T(8,128)(2,1)} %weights.1), custom_call_target="tpu_custom_call" | custom-call | tf_op jit(solution)/shard_map/residual_up/pallas_call | solution.py:68
  102.5 4.3 %all-to-all-start.2 = ((bf16[8,2,144,128]{3,2,1,0:T(8,128)(2,1)}), bf16[8,2,144,128]{3,2,1,0:T(8,128)(2,1)S(1)}, u32[]{:S(2)}, u32[]{:S(2)}) async-start(bf16[8,2,144,128]{3,2,1,0:T(8,128)(2,1)} %merge_heads.1), calls=%async_computation.2 | async-start | bytes 1179648 | tf_op jit(solution)/shard_map/all_to_all | solution.py:514
  108.4 8.2 %all-to-all-done.2.pieces = bf16[8,2,144,128]{3,2,1,0:T(8,128)(2,1)S(1)} async-done(((bf16[8,2,144,128]{3,2,1,0:T(8,128)(2,1)}), bf16[8,2,144,128]{3,2,1,0:T(8,128)(2,1)S(1)}, u32[]{:S(2)}, u32[]{:S(2)}) %all-to-all-start.2) | async-done | bytes 589856 | tf_op jit(solution)/shard_map/all_to_all | solution.py:514
  117.3 1.9 %collective-permute-start.14 = (bf16[288,128]{1,0:T(8,128)(2,1)S(1)}, bf16[288,128]{1,0:T(8,128)(2,1)S(1)}, u32[]{:S(2)}, u32[]{:S(2)}) collective-permute-start(bf16[288,128]{1,0:T(8,128)(2,1)S(1)} %get-tuple-element.89), channel_id=1, source_target_pairs={{0,8},{8,0},{1,9},{9,1},{2,10},{10,2},{3,11},{11,3},{4,12},{12,4},... | collective-permute-start | bytes 221192 | tf_op jit(solution)/shard_map/ppermute | solution.py:521
  119.3 2.1 %collective-permute-start.15 = (bf16[288,128]{1,0:T(8,128)(2,1)S(1)}, bf16[288,128]{1,0:T(8,128)(2,1)S(1)}, u32[]{:S(2)}, u32[]{:S(2)}) collective-permute-start(bf16[288,128]{1,0:T(8,128)(2,1)S(1)} %get-tuple-element.90), channel_id=1, source_target_pairs={{8,16},{24,32},{40,48},{56,64},{72,80},{88,96},{104,112},{120,128}... | collective-permute-start | bytes 221192 | tf_op jit(solution)/shard_map/ppermute | solution.py:523
  121.5 3.4 %collective-permute-done.15.far_up = bf16[288,128]{1,0:T(8,128)(2,1)S(1)} collective-permute-done((bf16[288,128]{1,0:T(8,128)(2,1)S(1)}, bf16[288,128]{1,0:T(8,128)(2,1)S(1)}, u32[]{:S(2)}, u32[]{:S(2)}) %collective-permute-start.15) | collective-permute-done | bytes 73760 | tf_op jit(solution)/shard_map/ppermute | solution.py:523
  124.9 2.8 %fine_stage.1 = (bf16[4,64,128]{2,1,0:T(8,128)(2,1)}, bf16[4,64,128]{2,1,0:T(8,128)(2,1)}, bf16[768,128]{1,0:T(8,128)(2,1)S(1)}) custom-call(s32[5]{0:T(128)S(1)} %convert_element_type.19.flags, bf16[2,144,128]{2,1,0:T(8,128)(2,1)S(1)} %get-tuple-element.88.own, bf16[288,128]{1,0:T(8,128)(2,1)S(1)} %collective-permute-done.14.near_up, ...), custom_call_target="tpu_custom_call" | custom-call | tf_op jit(solution)/shard_map/fine_stage/pallas_call | solution.py:403
  127.7 16.6 %all_to_all.31 = bf16[32,24,128]{2,1,0:T(8,128)(2,1)S(1)} all-to-all(bf16[32,24,128]{2,1,0:T(8,128)(2,1)S(1)} %bitcast.52), channel_id=1, replica_groups=mesh['xh'=2,'z'=8,'core'=2,'y'=4,'xl'=2] {'xh','core','y','xl'}, dimensions={0} | all-to-all | bytes 393216 | tf_op jit(solution)/shard_map/all_to_all | solution.py:529
  144.4 9.8 %all_to_all.32 = bf16[8,24,128]{2,1,0:T(8,128)(2,1)S(1)} all-to-all(bf16[8,24,128]{2,1,0:T(8,128)(2,1)S(1)} %broadcast_in_dim.4), channel_id=1, replica_groups=mesh['xh'=2,'z'=8,'core'=2,'y'=4,'xl'=2] {'z'}, dimensions={0} | all-to-all | bytes 98304 | tf_op jit(solution)/shard_map/all_to_all | solution.py:439
  154.2 13.5 %all_to_all.33 = bf16[32,24,128]{2,1,0:T(8,128)(2,1)S(1)} all-to-all(bf16[32,24,128]{2,1,0:T(8,128)(2,1)S(1)} %broadcast_in_dim.5), channel_id=1, replica_groups=mesh['xh'=2,'z'=8,'core'=2,'y'=4,'xl'=2] {'xh','core','y','xl'}, dimensions={0} | all-to-all | bytes 393216 | tf_op jit(solution)/shard_map/all_to_all | solution.py:439
  (72 shorter events, 9.9 us)
Async XLA Ops:
  0.6 10.0 %copy-start = (bf16[256,2048]{1,0:T(8,128)(2,1)S(1)}, bf16[256,2048]{1,0:T(8,128)(2,1)}, u32[]{:S(2)}) copy-start(bf16[256,2048]{1,0:T(8,128)(2,1)} %param.22) | copy-start | bytes 3145732
  3.2 20.5 %all-to-all-start = ((bf16[8,32,2048]{2,1,0:T(8,128)(2,1)}), bf16[8,32,2048]{2,1,0:T(8,128)(2,1)S(1)}, u32[]{:S(2)}, u32[]{:S(2)}) async-start(bf16[8,32,2048]{2,1,0:T(8,128)(2,1)} %bitcast.9), calls=%async_computation | async-start | bytes 2097152 | tf_op jit(solution)/shard_map/all_to_all | solution.py:469
  9.2 14.6 %copy-start.4 = (f32[2048]{0:T(1024)S(1)}, f32[2048]{0:T(1024)}, u32[]{:S(2)}) copy-start(f32[2048]{0:T(1024)} %param.18) | copy-start | bytes 24580
  23.7 20.8 %copy-start.5 = (bf16[2048,256]{1,0:T(8,128)(2,1)S(1)}, bf16[2048,256]{1,0:T(8,128)(2,1)}, u32[]{:S(2)}) copy-start(bf16[2048,256]{1,0:T(8,128)(2,1)} %param.20) | copy-start | bytes 3145732
  23.7 34.4 %copy-start.6 = (bf16[2048,256]{1,0:T(8,128)(2,1)S(1)}, bf16[2048,256]{1,0:T(8,128)(2,1)}, u32[]{:S(2)}) copy-start(bf16[2048,256]{1,0:T(8,128)(2,1)} %param.19) | copy-start | bytes 3145732
  45.0 10.4 %collective-permute-start.3 = (bf16[256,512]{1,0:T(8,128)(2,1)S(1)}, bf16[256,512]{1,0:T(8,128)(2,1)S(1)}, u32[]{:S(2)}, u32[]{:S(2)}) collective-permute-start(bf16[256,512]{1,0:T(8,128)(2,1)S(1)} %pad_maximum_fusion.1.refs_4_), channel_id=1, source_target_pairs={{0,16},{16,32},{32,48},{48,64},{64,80},{80,96},{96,112},{112,0},{1... | collective-permute-start | bytes 786440 | tf_op jit(solution)/shard_map/ppermute | solution.py:484
  46.7 8.7 %collective-permute-start.5 = (bf16[256,512]{1,0:T(8,128)(2,1)S(1)}, bf16[256,512]{1,0:T(8,128)(2,1)S(1)}, u32[]{:S(2)}, u32[]{:S(2)}) collective-permute-start(bf16[256,512]{1,0:T(8,128)(2,1)S(1)} %pad_maximum_fusion.1.refs_4_), channel_id=1, source_target_pairs={{0,112},{16,0},{32,16},{48,32},{64,48},{80,64},{96,80},{112,96},{1... | collective-permute-start | bytes 786440 | tf_op jit(solution)/shard_map/ppermute | solution.py:485
  55.4 17.0 %collective-permute-start.4 = (bf16[256,512]{1,0:T(8,128)(2,1)S(1)}, bf16[256,512]{1,0:T(8,128)(2,1)S(1)}, u32[]{:S(2)}, u32[]{:S(2)}) collective-permute-start(bf16[256,512]{1,0:T(8,128)(2,1)S(1)} %collective-permute-done.3.refs_5_), channel_id=1, source_target_pairs={{0,16},{16,32},{32,48},{48,64},{64,80},{80,96},{96,112},{112,0},{1... | collective-permute-start | bytes 786440 | tf_op jit(solution)/shard_map/ppermute | solution.py:489
  55.4 17.0 %collective-permute-start.6 = (bf16[256,512]{1,0:T(8,128)(2,1)S(1)}, bf16[256,512]{1,0:T(8,128)(2,1)S(1)}, u32[]{:S(2)}, u32[]{:S(2)}) collective-permute-start(bf16[256,512]{1,0:T(8,128)(2,1)S(1)} %collective-permute-done.5.refs_6_), channel_id=1, source_target_pairs={{0,112},{16,0},{32,16},{48,32},{64,48},{80,64},{96,80},{112,96},{1... | collective-permute-start | bytes 786440 | tf_op jit(solution)/shard_map/ppermute | solution.py:490
  58.5 6.3 %collective-permute-start = (bf16[256,256]{1,0:T(8,128)(2,1)S(1)}, bf16[256,256]{1,0:T(8,128)(2,1)S(1)}, u32[]{:S(2)}, u32[]{:S(2)}) collective-permute-start(bf16[256,256]{1,0:T(8,128)(2,1)S(1)} %convolution_convert_fusion.3.refs_0_), channel_id=1, source_target_pairs={{0,128},{8,136},{128,0},{136,8},{1,129},{9,137},{129,1},{137,9},{2... | collective-permute-start | bytes 393224 | tf_op jit(solution)/shard_map/ppermute | solution.py:487
  61.1 8.7 %collective-permute-start.1 = (bf16[256,256]{1,0:T(8,128)(2,1)S(1)}, bf16[256,256]{1,0:T(8,128)(2,1)S(1)}, u32[]{:S(2)}, u32[]{:S(2)}) collective-permute-start(bf16[256,256]{1,0:T(8,128)(2,1)S(1)} %convolution_convert_fusion.3.refs_0_), channel_id=1, source_target_pairs={{0,136},{8,128},{128,8},{136,0},{1,137},{9,129},{129,9},{137,1},{2... | collective-permute-start | bytes 393224 | tf_op jit(solution)/shard_map/ppermute | solution.py:487
  64.8 5.0 %collective-permute-start.2 = (bf16[256,256]{1,0:T(8,128)(2,1)S(1)}, bf16[256,256]{1,0:T(8,128)(2,1)S(1)}, u32[]{:S(2)}, u32[]{:S(2)}) collective-permute-start(bf16[256,256]{1,0:T(8,128)(2,1)S(1)} %convolution_convert_fusion.3.refs_0_), channel_id=1, source_target_pairs={{0,8},{8,0},{128,136},{136,128},{1,9},{9,1},{129,137},{137,129},{2... | collective-permute-start | bytes 393224 | tf_op jit(solution)/shard_map/ppermute | solution.py:487
  72.5 8.0 %collective-permute-start.7 = (bf16[256,512]{1,0:T(8,128)(2,1)S(1)}, bf16[256,512]{1,0:T(8,128)(2,1)S(1)}, u32[]{:S(2)}, u32[]{:S(2)}) collective-permute-start(bf16[256,512]{1,0:T(8,128)(2,1)S(1)} %collective-permute-done.4.refs_4_), channel_id=1, source_target_pairs={{0,16},{16,32},{32,48},{48,64},{64,80},{80,96},{96,112},{112,0},{1... | collective-permute-start | bytes 786440 | tf_op jit(solution)/shard_map/ppermute | solution.py:497
  72.6 7.9 %collective-permute-start.8 = (bf16[256,512]{1,0:T(8,128)(2,1)S(1)}, bf16[256,512]{1,0:T(8,128)(2,1)S(1)}, u32[]{:S(2)}, u32[]{:S(2)}) collective-permute-start(bf16[256,512]{1,0:T(8,128)(2,1)S(1)} %collective-permute-done.6.refs_5_), channel_id=1, source_target_pairs={{0,112},{16,0},{32,16},{48,32},{64,48},{80,64},{96,80},{112,96},{1... | collective-permute-start | bytes 786440 | tf_op jit(solution)/shard_map/ppermute | solution.py:498
  80.5 4.6 %collective-permute-start.10 = (bf16[128,512]{1,0:T(8,128)(2,1)S(1)}, bf16[128,512]{1,0:T(8,128)(2,1)S(1)}, u32[]{:S(2)}, u32[]{:S(2)}) collective-permute-start(bf16[128,512]{1,0:T(8,128)(2,1)S(1)} %slice.15), channel_id=1, source_target_pairs={{0,112},{16,0},{32,16},{48,32},{64,48},{80,64},{96,80},{112,96},{1... | collective-permute-start | bytes 393224 | tf_op jit(solution)/shard_map/ppermute | solution.py:498
  83.0 5.1 %collective-permute-start.9 = (bf16[128,512]{1,0:T(8,128)(2,1)S(1)}, bf16[128,512]{1,0:T(8,128)(2,1)S(1)}, u32[]{:S(2)}, u32[]{:S(2)}) collective-permute-start(bf16[128,512]{1,0:T(8,128)(2,1)S(1)} %slice.14), channel_id=1, source_target_pairs={{0,16},{16,32},{32,48},{48,64},{64,80},{80,96},{96,112},{112,0},{1... | collective-permute-start | bytes 393224 | tf_op jit(solution)/shard_map/ppermute | solution.py:497
  89.4 17.6 %copy-start.8 = (bf16[9,64,64]{2,1,0:T(8,128)(2,1)S(1)}, bf16[9,64,64]{2,1,0:T(8,128)(2,1)}, u32[]{:S(2)}) copy-start(bf16[9,64,64]{2,1,0:T(8,128)(2,1)} %param.26) | copy-start | bytes 221188
  89.4 10.6 %collective-permute-start.11 = (bf16[272,256]{1,0:T(8,128)(2,1)S(1)}, bf16[272,256]{1,0:T(8,128)(2,1)S(1)}, u32[]{:S(2)}, u32[]{:S(2)}) collective-permute-start(bf16[272,256]{1,0:T(8,128)(2,1)S(1)} %get-tuple-element.80), channel_id=1, source_target_pairs={{0,128},{8,136},{128,0},{136,8},{1,129},{9,137},{129,1},{137,9},{2... | collective-permute-start | bytes 417800 | tf_op jit(solution)/shard_map/ppermute | solution.py:510
  94.3 6.9 %collective-permute-start.12 = (bf16[272,256]{1,0:T(8,128)(2,1)S(1)}, bf16[272,256]{1,0:T(8,128)(2,1)S(1)}, u32[]{:S(2)}, u32[]{:S(2)}) collective-permute-start(bf16[272,256]{1,0:T(8,128)(2,1)S(1)} %get-tuple-element.81), channel_id=1, source_target_pairs={{0,136},{8,128},{128,8},{136,0},{1,137},{9,129},{129,9},{137,1},{2... | collective-permute-start | bytes 417800 | tf_op jit(solution)/shard_map/ppermute | solution.py:510
  96.3 4.9 %collective-permute-start.13 = (bf16[272,256]{1,0:T(8,128)(2,1)S(1)}, bf16[272,256]{1,0:T(8,128)(2,1)S(1)}, u32[]{:S(2)}, u32[]{:S(2)}) collective-permute-start(bf16[272,256]{1,0:T(8,128)(2,1)S(1)} %get-tuple-element.82), channel_id=1, source_target_pairs={{0,8},{8,0},{128,136},{136,128},{1,9},{9,1},{129,137},{137,129},{2... | collective-permute-start | bytes 417800 | tf_op jit(solution)/shard_map/ppermute | solution.py:510
  96.4 10.9 %copy-start.7 = (bf16[9,64,64]{2,1,0:T(8,128)(2,1)S(1)}, bf16[9,64,64]{2,1,0:T(8,128)(2,1)}, u32[]{:S(2)}) copy-start(bf16[9,64,64]{2,1,0:T(8,128)(2,1)} %param.24) | copy-start | bytes 221188
  99.9 16.8 %copy-start.1 = (bf16[4,64,128]{2,1,0:T(8,128)(2,1)S(1)}, bf16[4,64,128]{2,1,0:T(8,128)(2,1)}, u32[]{:S(2)}) copy-start(bf16[4,64,128]{2,1,0:T(8,128)(2,1)} %grad.1) | copy-start | bytes 196612
  99.9 21.5 %copy-start.9 = (f32[64]{0:T(128)S(1)}, f32[64]{0:T(128)}, u32[]{:S(2)}) copy-start(f32[64]{0:T(128)} %param.25) | copy-start | bytes 772
  99.9 25.0 %copy-start.2 = (bf16[144,1024]{1,0:T(8,128)(2,1)S(1)}, bf16[144,1024]{1,0:T(8,128)(2,1)}, u32[]{:S(2)}) copy-start(bf16[144,1024]{1,0:T(8,128)(2,1)} %constant.37.clone.spread) | copy-start | bytes 884740
  99.9 25.0 %copy-start.3 = (bf16[32,1024]{1,0:T(8,128)(2,1)S(1)}, bf16[32,1024]{1,0:T(8,128)(2,1)}, u32[]{:S(2)}) copy-start(bf16[32,1024]{1,0:T(8,128)(2,1)} %constant.38.clone.edges) | copy-start | bytes 196612
  102.5 14.2 %all-to-all-start.2 = ((bf16[8,2,144,128]{3,2,1,0:T(8,128)(2,1)}), bf16[8,2,144,128]{3,2,1,0:T(8,128)(2,1)S(1)}, u32[]{:S(2)}, u32[]{:S(2)}) async-start(bf16[8,2,144,128]{3,2,1,0:T(8,128)(2,1)} %merge_heads.1), calls=%async_computation.2 | async-start | bytes 1179648 | tf_op jit(solution)/shard_map/all_to_all | solution.py:514
  117.3 4.2 %collective-permute-start.14 = (bf16[288,128]{1,0:T(8,128)(2,1)S(1)}, bf16[288,128]{1,0:T(8,128)(2,1)S(1)}, u32[]{:S(2)}, u32[]{:S(2)}) collective-permute-start(bf16[288,128]{1,0:T(8,128)(2,1)S(1)} %get-tuple-element.89), channel_id=1, source_target_pairs={{0,8},{8,0},{1,9},{9,1},{2,10},{10,2},{3,11},{11,3},{4,12},{12,4},... | collective-permute-start | bytes 221192 | tf_op jit(solution)/shard_map/ppermute | solution.py:521
  119.3 5.7 %collective-permute-start.15 = (bf16[288,128]{1,0:T(8,128)(2,1)S(1)}, bf16[288,128]{1,0:T(8,128)(2,1)S(1)}, u32[]{:S(2)}, u32[]{:S(2)}) collective-permute-start(bf16[288,128]{1,0:T(8,128)(2,1)S(1)} %get-tuple-element.90), channel_id=1, source_target_pairs={{8,16},{24,32},{40,48},{56,64},{72,80},{88,96},{104,112},{120,128}... | collective-permute-start | bytes 221192 | tf_op jit(solution)/shard_map/ppermute | solution.py:523
